TPU v7x, 256 devices: a whole 4x4x8 slice. The times are simulated.
256 devices in a mesh: param: 16 (over x, y), space: 2 (over core), term: 8 (over z).
Axes of the slice: x: 4, y: 4, z: 8, core: 2. Of those that a mesh axis runs over, the one named last changes fastest.
Arguments:
- fields: float32 [128, 2, 8, 128, 128], P('param', None, None, 'space'), may hold values from -4 to 4
- library: int32 [168, 4], P('term'), may hold values from 0 to 6, as said below
- centers_x: int32 [16], replicated, may hold values from 0 to 127
- centers_y: int32 [16], replicated, may hold values from 0 to 127
- centers_t: int32 [4], replicated, may hold values from 0 to 7
- groups: int32 [168], replicated, may hold values from 0 to 23
Outputs:
- coefficients: float32 [128, 2, 168], P(('param', 'term'))
- misfit: float32 [128, 2, 168], P(('param', 'term'))
Inputs may be any that keep to these rules, and one draw needn't show every extreme that they name: `library`: each row (a, b, dx, dy) gives powers a and b of 0 to 6 and derivative orders dx and dy of 0 to 2; rows are distinct, and a = b = 0 only with dx = dy = 0.
All inputs are finite; a program needn't handle non-finite values.
Results may differ from a plain program's by a relative error of at most 0.00011.
Values sent between devices are 32-bit elements; how exact they have to be, the bound alone decides.
A program may use at most 64 MiB of HBM per device.

v0:
```python
import jax
import jax.numpy as jnp
from jax import lax
from jax.sharding import PartitionSpec as P

NX = 128
NY = 128
NT = 8
POWERS = 7
TERMS = 168
TESTS = 1024
RX = 16
RT = 4
GROUPS = 24
highest = lax.Precision.HIGHEST


def space_table(centers, first_row, row_count, extent):
    cell_index = first_row + jnp.arange(row_count, dtype=jnp.int32)
    offset = (cell_index[None, :] - centers[:, None] + extent // 2) % extent - extent // 2
    scaled = offset.astype(jnp.float32) / RX
    bump_base = 1.0 - scaled * scaled
    inside = jnp.abs(scaled) < 1.0
    cube = bump_base * bump_base * bump_base
    bump_value = jnp.where(inside, cube * bump_base, 0.0)
    bump_first = jnp.where(inside, 8.0 * scaled * cube / RX, 0.0)
    bump_second = jnp.where(
        inside, -8.0 * (cube - 6.0 * scaled * scaled * bump_base * bump_base) / (RX * RX), 0.0
    )
    return jnp.stack([bump_value, bump_first, bump_second])


def time_table(centers):
    step_index = jnp.arange(NT, dtype=jnp.int32)
    scaled = (step_index[None, :] - centers[:, None]).astype(jnp.float32) / RT
    bump_base = 1.0 - scaled * scaled
    inside = jnp.abs(scaled) < 1.0
    time_bump = jnp.where(inside, bump_base * bump_base, 0.0)
    time_slope = jnp.where(inside, 4.0 * scaled * bump_base / RT, 0.0)
    return (time_bump, time_slope)


def normalize(gram_matrix):
    diagonal = jnp.diagonal(gram_matrix, axis1=1, axis2=2)
    row_scale = jnp.sqrt(diagonal / TESTS + 1e-06)
    term_scale = row_scale[:, :TERMS]
    correlation = gram_matrix[:, :TERMS, :TERMS] / (
        TESTS * term_scale[:, :, None] * term_scale[:, None, :]
    )
    right_side = gram_matrix[:, TERMS:, :TERMS] / (
        TESTS * term_scale[:, None, :] * row_scale[:, TERMS:, None]
    )
    frobenius = jnp.sqrt(jnp.sum(correlation * correlation, axis=(1, 2)))
    return (correlation, right_side, frobenius)


def group_squares(values, onehot):
    return jnp.dot(jnp.sum(values * values, axis=(0, 1)), onehot, precision=highest)


def shrink(values, totals, onehot):
    threshold = 0.7 * jnp.sqrt(jnp.mean(totals))
    per_term = jnp.dot(onehot, totals, precision=highest)
    factor = jnp.maximum(0.0, 1.0 - threshold / jnp.sqrt(per_term + 1e-12))
    return values * factor


def correlate(correlation, values):
    return jnp.einsum("pij,psj->psi", correlation, values, precision=highest)


def body(fields, library, centers_x, centers_y, centers_t, groups):
    pgroup = fields.shape[0]
    tile_rows = fields.shape[3]
    space_count = lax.axis_size("space")
    term_count = lax.axis_size("term")
    local_terms = library.shape[0]
    row_count = local_terms + 2
    half_tests = TESTS // space_count
    y_table = space_table(centers_y, 0, NY, NY)
    time_bump, time_slope = time_table(centers_t)
    x_table = space_table(centers_x, lax.axis_index("space") * tile_rows, tile_rows, NX)
    share_rows = tile_rows // term_count
    share_start = lax.axis_index("term") * share_rows
    x_share = lax.dynamic_slice_in_dim(x_table[0], share_start, share_rows, 1)
    power_a = library[:, 0]
    power_b = library[:, 1]
    orders = jnp.arange(3, dtype=jnp.int32)
    pick_x = (library[:, 2][:, None] == orders[None, :]).astype(jnp.float32)
    pick_y = (library[:, 3][:, None] == orders[None, :]).astype(jnp.float32)
    x_pick = jnp.einsum("jd,dlx->jlx", pick_x, x_table, precision=highest)
    y_pick = jnp.einsum("jd,dky->jky", pick_y, y_table, precision=highest)

    def tile_integrals(field_pair):
        species_u = field_pair[0]
        species_v = field_pair[1]
        power_u = jnp.ones((local_terms,) + species_u.shape, jnp.float32)
        power_v = jnp.ones((local_terms,) + species_v.shape, jnp.float32)
        for degree in range(1, POWERS):
            power_u = power_u * jnp.where(
                power_a[:, None, None, None] >= degree, species_u[None], 1.0
            )
            power_v = power_v * jnp.where(
                power_b[:, None, None, None] >= degree, species_v[None], 1.0
            )
        monomial = power_u * power_v
        across_y = jnp.einsum("jtxy,jky->jtxk", monomial, y_pick, precision=highest)
        across_t = jnp.einsum("jtxk,rt->jrxk", across_y, time_bump, precision=highest)
        features = jnp.einsum("jrxk,jlx->jrkl", across_t, x_pick, precision=highest).reshape(
            local_terms, TESTS
        )
        share = lax.dynamic_slice_in_dim(field_pair, share_start, share_rows, 2)
        target_y = jnp.einsum("stxy,ky->stxk", share, y_table[0], precision=highest)
        targets = jnp.einsum(
            "stxk,rt,lx->srkl", target_y, time_slope, x_share, precision=highest
        ).reshape(2, TESTS)
        joined = jnp.concatenate([features, targets], axis=0).reshape(
            row_count, space_count, half_tests
        )
        return jnp.swapaxes(joined, 0, 1)

    def fill_param(index, buffer):
        field_pair = lax.dynamic_index_in_dim(fields, index, 0, keepdims=False)
        return lax.dynamic_update_slice_in_dim(
            buffer, tile_integrals(field_pair)[:, None], index, 1
        )

    buffer = jnp.zeros((space_count, pgroup, row_count, half_tests), jnp.float32)
    buffer = lax.fori_loop(0, pgroup, fill_param, buffer)
    received = lax.all_to_all(
        buffer.reshape(space_count * pgroup, row_count, half_tests),
        ("space", "term"),
        split_axis=0,
        concat_axis=1,
        tiled=True,
    )
    blocks = jnp.sum(received.reshape(space_count, term_count, row_count, half_tests), axis=0)
    features_half = blocks[:, :local_terms].reshape(term_count * local_terms, half_tests)
    targets_half = jnp.sum(blocks[:, local_terms:], axis=0)
    half_rows = jnp.concatenate([features_half, targets_half], axis=0)
    whole_rows = lax.all_gather(half_rows, "space", axis=1, tiled=True)
    gram_matrix = jnp.dot(whole_rows, whole_rows.T, precision=highest)[None]
    correlation, right_side, frobenius = normalize(gram_matrix)
    onehot = (groups[:, None] == jnp.arange(GROUPS, dtype=jnp.int32)[None, :]).astype(jnp.float32)
    largest = lax.pmax(jnp.max(frobenius), ("param", "term"))
    step_size = 1.0 / largest
    first_guess = step_size * right_side
    first_sq = lax.psum(group_squares(first_guess, onehot), ("param", "term"))
    first = shrink(first_guess, first_sq, onehot)
    second_guess = first - step_size * (correlate(correlation, first) - right_side)
    second_sq = lax.psum(group_squares(second_guess, onehot), ("param", "term"))
    second = shrink(second_guess, second_sq, onehot)
    coefficients = second / step_size
    misfit = right_side - correlate(correlation, second)
    return (coefficients, misfit)


def solution(mesh):
    return jax.shard_map(
        body,
        mesh=mesh,
        in_specs=(P("param", None, None, "space", None), P("term", None), P(), P(), P(), P()),
        out_specs=(P(("param", "term"), None, None), P(("param", "term"), None, None)),
        check_vma=False,
    )
```

profile of v0, /device:TPU:0, one launch (start us, length us, event | category | flops | bytes accessed | tf_op | source)
XLA Modules:
  0.0 1257.9 jit_solution(2309411352389409611)
XLA Ops:
  0.6 0.8 multiply_select_fusion.2
  1.5 0.7 fusion.127
  2.2 0.8 slice_bitcast_fusion.1
  3.4 0.8 multiply_select_fusion.5
  4.6 175.0 %while.18 = (s32[]{:T(128)}, f32[2,8,23,512]{3,0,2,1:T(2,128)S(1)}, s32[21,1]{0,1:T(1,128)S(1)}, f32[8,2,8,64,128]{4,3,2,1,0:T(8,128)}, s32[21,1]{0,1:T(1,128)S(...) while((s32[]{:T(128)}, f32[2,8,23,512]{3,0,2,1:T(2,128)S(1)}, ...), condition=%wide.region_1.2_spmd.clone.clone, body=%wide.region_0.1_spmd.clone.clone.sunk | while | flops 324181856 | bytes 4605749 | solution.py:129
  4.6 1.1 dynamic-slice_bitcast_fusion.6
  5.7 16.0 %fusion.203 = f32[21,8,64,16]{2,3,1,0:T(8,128)S(1)} fusion(f32[8,64,128]{2,1,0:T(8,128)S(1)} %get-tuple-element.566, f32[8,64,128]{2,1,0:T(8,128)S(1)} %get-tuple-element.567, pred[21]{0:T(512)(128)(4,1)S(1)} %get-tuple-element.568, pred[21]{0:T(512)(128)(4,1)S(1)} %get-tuple-element.569, pred[21]{0:T(512)(128)(4,1)S(1)} %get-tuple-element.570, ...), kind=kOutput, calls=%fused_computation.4.clone.1 | convolution fusion | flops 295895040 | bytes 1384700 | tf_op jit(solution)/shard_map/while/body/eval_jaxpr/jtxy,jky->jtxk/dot_general | solution.py:107
  21.7 1.6 fusion.204
  23.4 0.7 fusion.205
  24.1 0.4 concatenate.36
  24.5 0.9 dynamic-slice_bitcast_fusion.5
  26.5 1.1 dynamic-slice_bitcast_fusion.6
  27.6 16.0 %fusion.203 = f32[21,8,64,16]{2,3,1,0:T(8,128)S(1)} fusion(f32[8,64,128]{2,1,0:T(8,128)S(1)} %get-tuple-element.566, f32[8,64,128]{2,1,0:T(8,128)S(1)} %get-tuple-element.567, pred[21]{0:T(512)(128)(4,1)S(1)} %get-tuple-element.568, pred[21]{0:T(512)(128)(4,1)S(1)} %get-tuple-element.569, pred[21]{0:T(512)(128)(4,1)S(1)} %get-tuple-element.570, ...), kind=kOutput, calls=%fused_computation.4.clone.1 | convolution fusion | flops 295895040 | bytes 1384700 | tf_op jit(solution)/shard_map/while/body/eval_jaxpr/jtxy,jky->jtxk/dot_general | solution.py:107
  43.6 1.6 fusion.204
  45.2 0.7 fusion.205
  46.3 0.9 dynamic-slice_bitcast_fusion.5
  48.3 1.1 dynamic-slice_bitcast_fusion.6
  49.4 16.0 %fusion.203 = f32[21,8,64,16]{2,3,1,0:T(8,128)S(1)} fusion(f32[8,64,128]{2,1,0:T(8,128)S(1)} %get-tuple-element.566, f32[8,64,128]{2,1,0:T(8,128)S(1)} %get-tuple-element.567, pred[21]{0:T(512)(128)(4,1)S(1)} %get-tuple-element.568, pred[21]{0:T(512)(128)(4,1)S(1)} %get-tuple-element.569, pred[21]{0:T(512)(128)(4,1)S(1)} %get-tuple-element.570, ...), kind=kOutput, calls=%fused_computation.4.clone.1 | convolution fusion | flops 295895040 | bytes 1384700 | tf_op jit(solution)/shard_map/while/body/eval_jaxpr/jtxy,jky->jtxk/dot_general | solution.py:107
  65.4 1.6 fusion.204
  67.1 0.7 fusion.205
  67.8 0.4 concatenate.36
  68.2 0.9 dynamic-slice_bitcast_fusion.5
  70.2 1.1 dynamic-slice_bitcast_fusion.6
  71.3 16.0 %fusion.203 = f32[21,8,64,16]{2,3,1,0:T(8,128)S(1)} fusion(f32[8,64,128]{2,1,0:T(8,128)S(1)} %get-tuple-element.566, f32[8,64,128]{2,1,0:T(8,128)S(1)} %get-tuple-element.567, pred[21]{0:T(512)(128)(4,1)S(1)} %get-tuple-element.568, pred[21]{0:T(512)(128)(4,1)S(1)} %get-tuple-element.569, pred[21]{0:T(512)(128)(4,1)S(1)} %get-tuple-element.570, ...), kind=kOutput, calls=%fused_computation.4.clone.1 | convolution fusion | flops 295895040 | bytes 1384700 | tf_op jit(solution)/shard_map/while/body/eval_jaxpr/jtxy,jky->jtxk/dot_general | solution.py:107
  87.3 1.6 fusion.204
  88.9 0.7 fusion.205
  89.6 0.4 concatenate.36
  90.0 0.9 dynamic-slice_bitcast_fusion.5
  92.1 1.1 dynamic-slice_bitcast_fusion.6
  93.1 16.0 %fusion.203 = f32[21,8,64,16]{2,3,1,0:T(8,128)S(1)} fusion(f32[8,64,128]{2,1,0:T(8,128)S(1)} %get-tuple-element.566, f32[8,64,128]{2,1,0:T(8,128)S(1)} %get-tuple-element.567, pred[21]{0:T(512)(128)(4,1)S(1)} %get-tuple-element.568, pred[21]{0:T(512)(128)(4,1)S(1)} %get-tuple-element.569, pred[21]{0:T(512)(128)(4,1)S(1)} %get-tuple-element.570, ...), kind=kOutput, calls=%fused_computation.4.clone.1 | convolution fusion | flops 295895040 | bytes 1384700 | tf_op jit(solution)/shard_map/while/body/eval_jaxpr/jtxy,jky->jtxk/dot_general | solution.py:107
  109.1 1.6 fusion.204
  110.8 0.7 fusion.205
  111.5 0.4 concatenate.36
  111.9 0.9 dynamic-slice_bitcast_fusion.5
  113.9 1.1 dynamic-slice_bitcast_fusion.6
  115.0 16.0 %fusion.203 = f32[21,8,64,16]{2,3,1,0:T(8,128)S(1)} fusion(f32[8,64,128]{2,1,0:T(8,128)S(1)} %get-tuple-element.566, f32[8,64,128]{2,1,0:T(8,128)S(1)} %get-tuple-element.567, pred[21]{0:T(512)(128)(4,1)S(1)} %get-tuple-element.568, pred[21]{0:T(512)(128)(4,1)S(1)} %get-tuple-element.569, pred[21]{0:T(512)(128)(4,1)S(1)} %get-tuple-element.570, ...), kind=kOutput, calls=%fused_computation.4.clone.1 | convolution fusion | flops 295895040 | bytes 1384700 | tf_op jit(solution)/shard_map/while/body/eval_jaxpr/jtxy,jky->jtxk/dot_general | solution.py:107
  131.0 1.6 fusion.204
  132.6 0.7 fusion.205
  133.7 0.9 dynamic-slice_bitcast_fusion.5
  135.8 1.1 dynamic-slice_bitcast_fusion.6
  136.9 16.0 %fusion.203 = f32[21,8,64,16]{2,3,1,0:T(8,128)S(1)} fusion(f32[8,64,128]{2,1,0:T(8,128)S(1)} %get-tuple-element.566, f32[8,64,128]{2,1,0:T(8,128)S(1)} %get-tuple-element.567, pred[21]{0:T(512)(128)(4,1)S(1)} %get-tuple-element.568, pred[21]{0:T(512)(128)(4,1)S(1)} %get-tuple-element.569, pred[21]{0:T(512)(128)(4,1)S(1)} %get-tuple-element.570, ...), kind=kOutput, calls=%fused_computation.4.clone.1 | convolution fusion | flops 295895040 | bytes 1384700 | tf_op jit(solution)/shard_map/while/body/eval_jaxpr/jtxy,jky->jtxk/dot_general | solution.py:107
  152.8 1.6 fusion.204
  154.5 0.7 fusion.205
  155.6 0.9 dynamic-slice_bitcast_fusion.5
  157.6 1.1 dynamic-slice_bitcast_fusion.6
  158.7 16.0 %fusion.203 = f32[21,8,64,16]{2,3,1,0:T(8,128)S(1)} fusion(f32[8,64,128]{2,1,0:T(8,128)S(1)} %get-tuple-element.566, f32[8,64,128]{2,1,0:T(8,128)S(1)} %get-tuple-element.567, pred[21]{0:T(512)(128)(4,1)S(1)} %get-tuple-element.568, pred[21]{0:T(512)(128)(4,1)S(1)} %get-tuple-element.569, pred[21]{0:T(512)(128)(4,1)S(1)} %get-tuple-element.570, ...), kind=kOutput, calls=%fused_computation.4.clone.1 | convolution fusion | flops 295895040 | bytes 1384700 | tf_op jit(solution)/shard_map/while/body/eval_jaxpr/jtxy,jky->jtxk/dot_general | solution.py:107
  174.7 1.6 fusion.204
  176.3 0.7 fusion.205
  177.1 0.4 concatenate.36
  177.5 0.9 dynamic-slice_bitcast_fusion.5
  179.6 1.0 copy.33
  180.7 7.0 all-to-all-start
  187.6 20.5 %all-to-all-done = f32[16,23,512]{2,1,0:T(8,128)S(1)} async-done(((f32[16,23,512]{2,1,0:T(8,128)}), f32[16,23,512]{2,1,0:T(8,128)S(1)}, u32[]{:S(2)}, u32[]{:S(2)}) %all-to-all-start) | async-done | bytes 753696 | tf_op jit(solution)/shard_map/all_to_all | solution.py:130
  208.4 3.0 all_gather.3
  211.4 0.7 fusion.167
  212.2 2.8 gather_fusion
  215.0 0.7 multiply_reduce_fusion
  216.5 349.0 %pmax.7 = f32[]{:T(128)} all-reduce(f32[]{:T(128)S(6)} %sqrt.28), channel_id=1, replica_groups=mesh['param'=16,'space'=2,'term'=8] {'param','term'}, use_global_device_ids=true, to_apply=%region_5.6 | all-reduce | flops 1 | bytes 8 | tf_op jit(solution)/shard_map/pmax | solution.py:145
  566.5 342.2 %psum.14 = f32[24]{0:T(128)S(1)} all-reduce(f32[24]{0:T(128)S(1)} %convolution_bitcast_fusion.5), channel_id=1, replica_groups=mesh['param'=16,'space'=2,'term'=8] {'param','term'}, use_global_device_ids=true, to_apply=%region_7.8 | all-reduce | flops 24 | bytes 192 | tf_op jit(solution)/shard_map/psum | solution.py:148
  908.7 0.6 reduce_sum.67
  910.7 344.2 %psum.15 = f32[24]{0:T(128)S(1)} all-reduce(f32[24]{0:T(128)S(1)} %convolution_bitcast_fusion.4), channel_id=1, replica_groups=mesh['param'=16,'space'=2,'term'=8] {'param','term'}, use_global_device_ids=true, to_apply=%region_10.11 | all-reduce | flops 24 | bytes 192 | tf_op jit(solution)/shard_map/psum | solution.py:151
  1254.9 0.6 reduce_sum.69
  1256.5 0.8 fusion.112
  1257.4 0.6 multiply_divide_fusion
  (116 shorter events, 11.5 us)
Async XLA Ops:
  5.7 16.0 %copy-start = (s32[4]{0:T(128)S(1)}, s32[4]{0:T(128)}, u32[]{:S(2)}) copy-start(s32[4]{0:T(128)} %get-tuple-element.619) | copy-start | bytes 52 | tf_op jit(solution)/shard_map/while
  21.7 3.7 copy-start.1
  27.6 16.0 %copy-start = (s32[4]{0:T(128)S(1)}, s32[4]{0:T(128)}, u32[]{:S(2)}) copy-start(s32[4]{0:T(128)} %get-tuple-element.619) | copy-start | bytes 52 | tf_op jit(solution)/shard_map/while
  43.5 3.7 copy-start.1
  49.4 16.0 %copy-start = (s32[4]{0:T(128)S(1)}, s32[4]{0:T(128)}, u32[]{:S(2)}) copy-start(s32[4]{0:T(128)} %get-tuple-element.619) | copy-start | bytes 52 | tf_op jit(solution)/shard_map/while
  65.4 3.7 copy-start.1
  71.3 16.0 %copy-start = (s32[4]{0:T(128)S(1)}, s32[4]{0:T(128)}, u32[]{:S(2)}) copy-start(s32[4]{0:T(128)} %get-tuple-element.619) | copy-start | bytes 52 | tf_op jit(solution)/shard_map/while
  87.2 3.7 copy-start.1
  93.1 16.0 %copy-start = (s32[4]{0:T(128)S(1)}, s32[4]{0:T(128)}, u32[]{:S(2)}) copy-start(s32[4]{0:T(128)} %get-tuple-element.619) | copy-start | bytes 52 | tf_op jit(solution)/shard_map/while
  109.1 3.7 copy-start.1
  115.0 16.0 %copy-start = (s32[4]{0:T(128)S(1)}, s32[4]{0:T(128)}, u32[]{:S(2)}) copy-start(s32[4]{0:T(128)} %get-tuple-element.619) | copy-start | bytes 52 | tf_op jit(solution)/shard_map/while
  131.0 3.7 copy-start.1
  136.8 16.0 %copy-start = (s32[4]{0:T(128)S(1)}, s32[4]{0:T(128)}, u32[]{:S(2)}) copy-start(s32[4]{0:T(128)} %get-tuple-element.619) | copy-start | bytes 52 | tf_op jit(solution)/shard_map/while
  152.8 3.7 copy-start.1
  158.7 16.0 %copy-start = (s32[4]{0:T(128)S(1)}, s32[4]{0:T(128)}, u32[]{:S(2)}) copy-start(s32[4]{0:T(128)} %get-tuple-element.619) | copy-start | bytes 52 | tf_op jit(solution)/shard_map/while
  174.7 3.7 copy-start.1
  180.7 385.7 %copy-start.2 = (s32[168]{0:T(256)S(1)}, s32[168]{0:T(256)}, u32[]{:S(2)}) copy-start(s32[168]{0:T(256)} %param.13) | copy-start | bytes 2020
  180.7 27.5 %all-to-all-start = ((f32[16,23,512]{2,1,0:T(8,128)}), f32[16,23,512]{2,1,0:T(8,128)S(1)}, u32[]{:S(2)}, u32[]{:S(2)}) async-start(f32[16,23,512]{2,1,0:T(8,128)} %bitcast.5), calls=%async_computation | async-start | bytes 1572864 | tf_op jit(solution)/shard_map/all_to_all | solution.py:130
where the time goes:
time: 1260 us
  blocking collectives  1040 us (83%)
  matrix products  157 us (12%)
  local copies, waits for them, and re-layouts  24.8 us (2%)
  waiting for transfers between devices  20.5 us (2%)
    pmax x1, blocking collectives, body(): largest = lax.pmax(jnp.max(frobenius), ('param', 'term'))  349 us
    psum x1, blocking collectives, body(): second_sq = lax.psum(group_squares(second_guess, onehot), ('param', 'term'))  344 us
    psum x1, blocking collectives, body(): first_sq = lax.psum(group_squares(first_guess, onehot), ('param', 'term'))  342 us
    dot_general x8, matrix products, tile_integrals(): across_y = jnp.einsum('jtxy,jky->jtxk', monomial, y_pick, precision=highest)  128 us
  transfers between devices with their start and end apart: 1, of which 1 were waited for; matrix products, arithmetic and copies ran while one was open for 0% of the time, Pallas kernels for 0%

commit v1 on v0

--- a/solution.py
+++ b/solution.py
@@ -148,7 +148,7 @@
     first_sq = lax.psum(group_squares(first_guess, onehot), ("param", "term"))
     first = shrink(first_guess, first_sq, onehot)
     second_guess = first - step_size * (correlate(correlation, first) - right_side)
-    second_sq = lax.psum(group_squares(second_guess, onehot), ("param", "term"))
+    second_sq = lax.psum(lax.psum(group_squares(second_guess, onehot), "param"), "term")
     second = shrink(second_guess, second_sq, onehot)
     coefficients = second / step_size
     misfit = right_side - correlate(correlation, second)

time: 1260 us -> 968 us (0.77)
  blocking collectives: 1040 us -> 746 us
    psum x1 -> x2, blocking collectives: 344 us -> 52.2 us  [the longest x1 35.5 us: body(): lax.psum(group_squares(second_guess, onehot), 'param')]
where the time goes in v1:
time: 968 us; the launch traced here: 966 us
  blocking collectives  746 us (77%)
  matrix products  157 us (16%)
  local copies, waits for them, and re-layouts  24.8 us (3%)
  waiting for transfers between devices  20.5 us (2%)
    pmax x1, blocking collectives, body(): largest = lax.pmax(jnp.max(frobenius), ('param', 'term'))  349 us
    psum x1, blocking collectives, body(): first_sq = lax.psum(group_squares(first_guess, onehot), ('param', 'term'))  342 us
    dot_general x8, matrix products, tile_integrals(): across_y = jnp.einsum('jtxy,jky->jtxk', monomial, y_pick, precision=highest)  128 us
    psum x1, blocking collectives, body(): lax.psum(group_squares(second_guess, onehot), 'param')  35.5 us
    all_to_all x1, waiting for transfers between devices, body(): lax.all_to_all(buffer.reshape(space_count * pgroup, row_count, half_tests...  20.5 us
  transfers between devices with their start and end apart: 1, of which 1 were waited for; matrix products, arithmetic and copies ran while one was open for 0% of the time, Pallas kernels for 0%

profile of v1, /device:TPU:0, one launch (start us, length us, event | category | flops | bytes accessed | tf_op | source)
XLA Modules:
  0.0 965.9 jit_solution(1410907970549381623)
XLA Ops:
  0.6 0.8 multiply_select_fusion.2
  1.5 0.7 fusion.127
  2.2 0.8 slice_bitcast_fusion.1
  3.4 0.8 multiply_select_fusion.5
  4.6 175.0 %while.18 = (s32[]{:T(128)}, f32[2,8,23,512]{3,0,2,1:T(2,128)S(1)}, s32[21,1]{0,1:T(1,128)S(1)}, f32[8,2,8,64,128]{4,3,2,1,0:T(8,128)}, s32[21,1]{0,1:T(1,128)S(...) while((s32[]{:T(128)}, f32[2,8,23,512]{3,0,2,1:T(2,128)S(1)}, ...), condition=%wide.region_1.2_spmd.clone.clone, body=%wide.region_0.1_spmd.clone.clone.sunk | while | flops 324181856 | bytes 4605749 | solution.py:129
  4.6 1.1 dynamic-slice_bitcast_fusion.6
  5.7 16.0 %fusion.203 = f32[21,8,64,16]{2,3,1,0:T(8,128)S(1)} fusion(f32[8,64,128]{2,1,0:T(8,128)S(1)} %get-tuple-element.566, f32[8,64,128]{2,1,0:T(8,128)S(1)} %get-tuple-element.567, pred[21]{0:T(512)(128)(4,1)S(1)} %get-tuple-element.568, pred[21]{0:T(512)(128)(4,1)S(1)} %get-tuple-element.569, pred[21]{0:T(512)(128)(4,1)S(1)} %get-tuple-element.570, ...), kind=kOutput, calls=%fused_computation.4.clone.1 | convolution fusion | flops 295895040 | bytes 1384700 | tf_op jit(solution)/shard_map/while/body/eval_jaxpr/jtxy,jky->jtxk/dot_general | solution.py:107
  21.7 1.6 fusion.204
  23.4 0.7 fusion.205
  24.1 0.4 concatenate.36
  24.5 0.9 dynamic-slice_bitcast_fusion.5
  26.5 1.1 dynamic-slice_bitcast_fusion.6
  27.6 16.0 %fusion.203 = f32[21,8,64,16]{2,3,1,0:T(8,128)S(1)} fusion(f32[8,64,128]{2,1,0:T(8,128)S(1)} %get-tuple-element.566, f32[8,64,128]{2,1,0:T(8,128)S(1)} %get-tuple-element.567, pred[21]{0:T(512)(128)(4,1)S(1)} %get-tuple-element.568, pred[21]{0:T(512)(128)(4,1)S(1)} %get-tuple-element.569, pred[21]{0:T(512)(128)(4,1)S(1)} %get-tuple-element.570, ...), kind=kOutput, calls=%fused_computation.4.clone.1 | convolution fusion | flops 295895040 | bytes 1384700 | tf_op jit(solution)/shard_map/while/body/eval_jaxpr/jtxy,jky->jtxk/dot_general | solution.py:107
  43.6 1.6 fusion.204
  45.2 0.7 fusion.205
  46.3 0.9 dynamic-slice_bitcast_fusion.5
  48.3 1.1 dynamic-slice_bitcast_fusion.6
  49.4 16.0 %fusion.203 = f32[21,8,64,16]{2,3,1,0:T(8,128)S(1)} fusion(f32[8,64,128]{2,1,0:T(8,128)S(1)} %get-tuple-element.566, f32[8,64,128]{2,1,0:T(8,128)S(1)} %get-tuple-element.567, pred[21]{0:T(512)(128)(4,1)S(1)} %get-tuple-element.568, pred[21]{0:T(512)(128)(4,1)S(1)} %get-tuple-element.569, pred[21]{0:T(512)(128)(4,1)S(1)} %get-tuple-element.570, ...), kind=kOutput, calls=%fused_computation.4.clone.1 | convolution fusion | flops 295895040 | bytes 1384700 | tf_op jit(solution)/shard_map/while/body/eval_jaxpr/jtxy,jky->jtxk/dot_general | solution.py:107
  65.4 1.6 fusion.204
  67.1 0.7 fusion.205
  67.8 0.4 concatenate.36
  68.2 0.9 dynamic-slice_bitcast_fusion.5
  70.2 1.1 dynamic-slice_bitcast_fusion.6
  71.3 16.0 %fusion.203 = f32[21,8,64,16]{2,3,1,0:T(8,128)S(1)} fusion(f32[8,64,128]{2,1,0:T(8,128)S(1)} %get-tuple-element.566, f32[8,64,128]{2,1,0:T(8,128)S(1)} %get-tuple-element.567, pred[21]{0:T(512)(128)(4,1)S(1)} %get-tuple-element.568, pred[21]{0:T(512)(128)(4,1)S(1)} %get-tuple-element.569, pred[21]{0:T(512)(128)(4,1)S(1)} %get-tuple-element.570, ...), kind=kOutput, calls=%fused_computation.4.clone.1 | convolution fusion | flops 295895040 | bytes 1384700 | tf_op jit(solution)/shard_map/while/body/eval_jaxpr/jtxy,jky->jtxk/dot_general | solution.py:107
  87.3 1.6 fusion.204
  88.9 0.7 fusion.205
  89.6 0.4 concatenate.36
  90.0 0.9 dynamic-slice_bitcast_fusion.5
  92.1 1.1 dynamic-slice_bitcast_fusion.6
  93.1 16.0 %fusion.203 = f32[21,8,64,16]{2,3,1,0:T(8,128)S(1)} fusion(f32[8,64,128]{2,1,0:T(8,128)S(1)} %get-tuple-element.566, f32[8,64,128]{2,1,0:T(8,128)S(1)} %get-tuple-element.567, pred[21]{0:T(512)(128)(4,1)S(1)} %get-tuple-element.568, pred[21]{0:T(512)(128)(4,1)S(1)} %get-tuple-element.569, pred[21]{0:T(512)(128)(4,1)S(1)} %get-tuple-element.570, ...), kind=kOutput, calls=%fused_computation.4.clone.1 | convolution fusion | flops 295895040 | bytes 1384700 | tf_op jit(solution)/shard_map/while/body/eval_jaxpr/jtxy,jky->jtxk/dot_general | solution.py:107
  109.1 1.6 fusion.204
  110.8 0.7 fusion.205
  111.5 0.4 concatenate.36
  111.9 0.9 dynamic-slice_bitcast_fusion.5
  113.9 1.1 dynamic-slice_bitcast_fusion.6
  115.0 16.0 %fusion.203 = f32[21,8,64,16]{2,3,1,0:T(8,128)S(1)} fusion(f32[8,64,128]{2,1,0:T(8,128)S(1)} %get-tuple-element.566, f32[8,64,128]{2,1,0:T(8,128)S(1)} %get-tuple-element.567, pred[21]{0:T(512)(128)(4,1)S(1)} %get-tuple-element.568, pred[21]{0:T(512)(128)(4,1)S(1)} %get-tuple-element.569, pred[21]{0:T(512)(128)(4,1)S(1)} %get-tuple-element.570, ...), kind=kOutput, calls=%fused_computation.4.clone.1 | convolution fusion | flops 295895040 | bytes 1384700 | tf_op jit(solution)/shard_map/while/body/eval_jaxpr/jtxy,jky->jtxk/dot_general | solution.py:107
  131.0 1.6 fusion.204
  132.6 0.7 fusion.205
  133.7 0.9 dynamic-slice_bitcast_fusion.5
  135.8 1.1 dynamic-slice_bitcast_fusion.6
  136.9 16.0 %fusion.203 = f32[21,8,64,16]{2,3,1,0:T(8,128)S(1)} fusion(f32[8,64,128]{2,1,0:T(8,128)S(1)} %get-tuple-element.566, f32[8,64,128]{2,1,0:T(8,128)S(1)} %get-tuple-element.567, pred[21]{0:T(512)(128)(4,1)S(1)} %get-tuple-element.568, pred[21]{0:T(512)(128)(4,1)S(1)} %get-tuple-element.569, pred[21]{0:T(512)(128)(4,1)S(1)} %get-tuple-element.570, ...), kind=kOutput, calls=%fused_computation.4.clone.1 | convolution fusion | flops 295895040 | bytes 1384700 | tf_op jit(solution)/shard_map/while/body/eval_jaxpr/jtxy,jky->jtxk/dot_general | solution.py:107
  152.8 1.6 fusion.204
  154.5 0.7 fusion.205
  155.6 0.9 dynamic-slice_bitcast_fusion.5
  157.6 1.1 dynamic-slice_bitcast_fusion.6
  158.7 16.0 %fusion.203 = f32[21,8,64,16]{2,3,1,0:T(8,128)S(1)} fusion(f32[8,64,128]{2,1,0:T(8,128)S(1)} %get-tuple-element.566, f32[8,64,128]{2,1,0:T(8,128)S(1)} %get-tuple-element.567, pred[21]{0:T(512)(128)(4,1)S(1)} %get-tuple-element.568, pred[21]{0:T(512)(128)(4,1)S(1)} %get-tuple-element.569, pred[21]{0:T(512)(128)(4,1)S(1)} %get-tuple-element.570, ...), kind=kOutput, calls=%fused_computation.4.clone.1 | convolution fusion | flops 295895040 | bytes 1384700 | tf_op jit(solution)/shard_map/while/body/eval_jaxpr/jtxy,jky->jtxk/dot_general | solution.py:107
  174.7 1.6 fusion.204
  176.3 0.7 fusion.205
  177.5 0.9 dynamic-slice_bitcast_fusion.5
  179.6 1.0 copy.33
  180.7 7.0 all-to-all-start
  187.6 20.5 %all-to-all-done = f32[16,23,512]{2,1,0:T(8,128)S(1)} async-done(((f32[16,23,512]{2,1,0:T(8,128)}), f32[16,23,512]{2,1,0:T(8,128)S(1)}, u32[]{:S(2)}, u32[]{:S(2)}) %all-to-all-start) | async-done | bytes 753696 | tf_op jit(solution)/shard_map/all_to_all | solution.py:130
  208.4 3.0 all_gather.3
  211.4 0.7 fusion.167
  212.2 2.8 gather_fusion
  215.0 0.7 multiply_reduce_fusion
  216.5 349.0 %pmax.7 = f32[]{:T(128)} all-reduce(f32[]{:T(128)S(6)} %sqrt.28), channel_id=1, replica_groups=mesh['param'=16,'space'=2,'term'=8] {'param','term'}, use_global_device_ids=true, to_apply=%region_5.6 | all-reduce | flops 1 | bytes 8 | tf_op jit(solution)/shard_map/pmax | solution.py:145
  566.5 342.2 %psum.21 = f32[24]{0:T(128)S(1)} all-reduce(f32[24]{0:T(128)S(1)} %convolution_bitcast_fusion.5), channel_id=1, replica_groups=mesh['param'=16,'space'=2,'term'=8] {'param','term'}, use_global_device_ids=true, to_apply=%region_7.8 | all-reduce | flops 24 | bytes 192 | tf_op jit(solution)/shard_map/psum | solution.py:148
  908.7 0.6 reduce_sum.67
  910.7 35.5 %psum.22 = f32[24]{0:T(128)S(1)} all-reduce(f32[24]{0:T(128)S(1)} %convolution_bitcast_fusion.4), channel_id=1, replica_groups=mesh['param'=16,'space'=2,'term'=8] {'param'}, use_global_device_ids=true, to_apply=%region_10.11 | all-reduce | flops 24 | bytes 192 | tf_op jit(solution)/shard_map/psum | solution.py:151
  946.2 16.7 %psum.23 = f32[24]{0:T(128)S(1)} all-reduce(f32[24]{0:T(128)S(1)} %psum.22), channel_id=1, replica_groups=mesh['param'=16,'space'=2,'term'=8] {'term'}, use_global_device_ids=true, to_apply=%region_11.12 | all-reduce | flops 24 | bytes 192 | tf_op jit(solution)/shard_map/psum | solution.py:151
  962.9 0.6 reduce_sum.69
  964.5 0.8 fusion.112
  965.3 0.6 multiply_divide_fusion
  (117 shorter events, 11.9 us)
Async XLA Ops:
  5.7 16.0 %copy-start = (s32[4]{0:T(128)S(1)}, s32[4]{0:T(128)}, u32[]{:S(2)}) copy-start(s32[4]{0:T(128)} %get-tuple-element.619) | copy-start | bytes 52 | tf_op jit(solution)/shard_map/while
  21.7 3.7 copy-start.1
  27.6 16.0 %copy-start = (s32[4]{0:T(128)S(1)}, s32[4]{0:T(128)}, u32[]{:S(2)}) copy-start(s32[4]{0:T(128)} %get-tuple-element.619) | copy-start | bytes 52 | tf_op jit(solution)/shard_map/while
  43.5 3.7 copy-start.1
  49.4 16.0 %copy-start = (s32[4]{0:T(128)S(1)}, s32[4]{0:T(128)}, u32[]{:S(2)}) copy-start(s32[4]{0:T(128)} %get-tuple-element.619) | copy-start | bytes 52 | tf_op jit(solution)/shard_map/while
  65.4 3.7 copy-start.1
  71.3 16.0 %copy-start = (s32[4]{0:T(128)S(1)}, s32[4]{0:T(128)}, u32[]{:S(2)}) copy-start(s32[4]{0:T(128)} %get-tuple-element.619) | copy-start | bytes 52 | tf_op jit(solution)/shard_map/while
  87.2 3.7 copy-start.1
  93.1 16.0 %copy-start = (s32[4]{0:T(128)S(1)}, s32[4]{0:T(128)}, u32[]{:S(2)}) copy-start(s32[4]{0:T(128)} %get-tuple-element.619) | copy-start | bytes 52 | tf_op jit(solution)/shard_map/while
  109.1 3.7 copy-start.1
  115.0 16.0 %copy-start = (s32[4]{0:T(128)S(1)}, s32[4]{0:T(128)}, u32[]{:S(2)}) copy-start(s32[4]{0:T(128)} %get-tuple-element.619) | copy-start | bytes 52 | tf_op jit(solution)/shard_map/while
  131.0 3.7 copy-start.1
  136.8 16.0 %copy-start = (s32[4]{0:T(128)S(1)}, s32[4]{0:T(128)}, u32[]{:S(2)}) copy-start(s32[4]{0:T(128)} %get-tuple-element.619) | copy-start | bytes 52 | tf_op jit(solution)/shard_map/while
  152.8 3.7 copy-start.1
  158.7 16.0 %copy-start = (s32[4]{0:T(128)S(1)}, s32[4]{0:T(128)}, u32[]{:S(2)}) copy-start(s32[4]{0:T(128)} %get-tuple-element.619) | copy-start | bytes 52 | tf_op jit(solution)/shard_map/while
  174.7 3.7 copy-start.1
  180.7 385.7 %copy-start.2 = (s32[168]{0:T(256)S(1)}, s32[168]{0:T(256)}, u32[]{:S(2)}) copy-start(s32[168]{0:T(256)} %param.13) | copy-start | bytes 2020
  180.7 27.5 %all-to-all-start = ((f32[16,23,512]{2,1,0:T(8,128)}), f32[16,23,512]{2,1,0:T(8,128)S(1)}, u32[]{:S(2)}, u32[]{:S(2)}) async-start(f32[16,23,512]{2,1,0:T(8,128)} %bitcast.5), calls=%async_computation | async-start | bytes 1572864 | tf_op jit(solution)/shard_map/all_to_all | solution.py:130
